TPU v7x, 32 devices: a whole 2x2x4 slice. The times are simulated.
32 devices in a mesh: batch: 16 (over z, y, core), tm: 2 (over x).
Axes of the slice: x: 2, y: 2, z: 4, core: 2. Of those that a mesh axis runs over, the one named last changes fastest.
Arguments:
- ref_rows: bfloat16 [8192, 1024], P(('batch', 'tm')), may hold values from -6 to 6
- neg_rows: bfloat16 [2048, 1024], P(('batch', 'tm')), may hold values from -6 to 6
- recording: bfloat16 [1024, 1024], P('tm'), may hold values from -6 to 6
- pos_owner: int32 [8192, 1], P(('batch', 'tm')), may hold values from 0 to 1; in each aligned block of 256 rows (0 to 255, 256 to 511, ...) at most 256 rows name the same one
- pos_row: int32 [8192], P(('batch', 'tm')), may hold values from 0 to 511
- ref_animal: int32 [8192], P(('batch', 'tm')), may hold values from 0 to 7
- neg_animal: int32 [2048], P(('batch', 'tm')), may hold values from 0 to 7
- w_in: bfloat16 [1024, 512], replicated, may hold values from -0.1875 to 0.1875
- bias_animal: float32 [8, 512], replicated, may hold values from -5 to 5
- w_out: bfloat16 [512, 128], replicated, may hold values from -0.25 to 0.25
Outputs:
- ref_loss: float32 [8192], P(('batch', 'tm'))
- grad_w_in: bfloat16 [1024, 512], replicated
- grad_w_out: float32 [512, 128], replicated
- grad_bias: float32 [8, 512], replicated
Inputs may be any that keep to these rules, and one draw needn't show every extreme that they name: `pos_owner`: among the 256 references of one device at most 256 name one owner, and in every draw some owner is named by exactly 256 of them.
All inputs are finite; a program needn't handle non-finite values.
Results may differ from a plain program's by a relative error of at most 0.0069.
Values may be sent and summed in bfloat16 or wider, within the bound.
No kernel may reach another device: no remote copies, remote signals or barrier semaphores. Data moves between devices by JAX's collectives and lax.ppermute only.
A program may use at most 64 MiB of HBM per device.

v0:
```python
import math
import jax
import jax.numpy as jnp
from jax import lax
from jax.sharding import PartitionSpec as P

logit_sharpness_divisor = 0.1
shift_bound = 10.0
epsilon = 1e-06


def encode_rows(samples, animal_ids, w_in, bias_animal, w_out):
    animals = bias_animal.shape[0]
    one_hot = (animal_ids[:, None] == jnp.arange(animals, dtype=jnp.int32)[None, :]).astype(
        jnp.float32
    )
    pre_act = jnp.dot(samples, w_in, preferred_element_type=jnp.float32) + jnp.dot(
        one_hot, bias_animal, precision=lax.Precision.HIGHEST
    )
    hidden = jax.nn.gelu(pre_act).astype(jnp.bfloat16)
    latent = jnp.dot(hidden, w_out, preferred_element_type=jnp.float32)
    radius = jnp.sqrt(jnp.sum(latent * latent, axis=1, keepdims=True) + epsilon)
    unit_vec = (latent / radius).astype(jnp.bfloat16)
    return (pre_act, hidden, latent, radius, unit_vec)


def on_device(
    ref_rows,
    neg_rows,
    recording,
    pos_owner,
    pos_row,
    ref_animal,
    neg_animal,
    w_in,
    bias_animal,
    w_out,
):
    anchors_each_processor = ref_rows.shape[0]
    negs_dev = neg_rows.shape[0]
    embed_width = w_out.shape[1]
    holder_processors = lax.axis_size("tm")
    minibatch_clusters = lax.axis_size("batch")
    capacity = 2 * anchors_each_processor // holder_processors
    first_enc = encode_rows(
        jnp.concatenate([ref_rows, neg_rows], 0),
        jnp.concatenate([ref_animal, neg_animal]),
        w_in,
        bias_animal,
        w_out,
    )
    reference_unit_vector = first_enc[4][:anchors_each_processor]
    neg_unit = first_enc[4][anchors_each_processor:]
    pool = lax.all_gather(neg_unit, "batch", axis=0, tiled=True)
    owner_ids = pos_owner[:, 0]
    owner_hot = (
        owner_ids[:, None] == jnp.arange(holder_processors, dtype=jnp.int32)[None, :]
    ).astype(jnp.int32)
    slot_ids = jnp.sum((jnp.cumsum(owner_hot, axis=0) - owner_hot) * owner_hot, axis=1)
    places = owner_ids * capacity + slot_ids
    requests = (
        jnp.zeros((holder_processors * capacity,), jnp.int32)
        .at[places]
        .set(pos_row)
        .reshape(holder_processors, capacity)
    )
    asked = lax.all_to_all(requests, "tm", split_axis=0, concat_axis=0, tiled=True)
    found = jnp.take(recording, asked.reshape(-1), axis=0)
    found = found.reshape(asked.shape[0], asked.shape[1], recording.shape[1])
    arrived = lax.all_to_all(found, "tm", split_axis=0, concat_axis=0, tiled=True)
    pos_rows = jnp.take(
        arrived.reshape(holder_processors * capacity, recording.shape[1]), places, axis=0
    )
    second_enc = encode_rows(pos_rows, ref_animal, w_in, bias_animal, w_out)
    positive_unit_vector = second_enc[4]
    group = math.gcd(minibatch_clusters, max(1, 2048 // negs_dev))
    width = group * negs_dev
    blocks = minibatch_clusters // group
    matching_similarity = (
        jnp.sum(
            reference_unit_vector.astype(jnp.float32) * positive_unit_vector.astype(jnp.float32),
            axis=1,
        )
        / logit_sharpness_divisor
    )

    def block_scores(start):
        block_part = lax.dynamic_slice_in_dim(pool, start, width, 0)
        similarity_table = (
            jnp.einsum(
                "ka,sa->ks", reference_unit_vector, block_part, preferred_element_type=jnp.float32
            )
            / logit_sharpness_divisor
        )
        return (block_part, similarity_table)

    def add_exp(step_index, running):
        block_part, similarity_table = block_scores(step_index * width)
        return running + jnp.sum(jnp.exp(similarity_table - shift_bound), axis=1)

    normalizer = lax.fori_loop(0, blocks, add_exp, jnp.exp(matching_similarity - shift_bound))

    def add_pull(step_index, running):
        block_part, similarity_table = block_scores(step_index * width)
        weights = (jnp.exp(similarity_table - shift_bound) / normalizer[:, None]).astype(
            jnp.bfloat16
        )
        return running + jnp.dot(weights, block_part, preferred_element_type=jnp.float32)

    pulled = lax.fori_loop(
        0, blocks, add_pull, jnp.zeros((anchors_each_processor, embed_width), jnp.float32)
    )
    ref_loss = jnp.log(normalizer) + shift_bound - matching_similarity
    pos_prob = jnp.exp(matching_similarity - shift_bound) / normalizer
    reciprocal_factor = (
        float(anchors_each_processor * minibatch_clusters * holder_processors) ** (-0.5)
        / logit_sharpness_divisor
    )
    grad_ref = reciprocal_factor * (
        pulled + (pos_prob - 1.0)[:, None] * positive_unit_vector.astype(jnp.float32)
    )
    grad_pos = (
        reciprocal_factor * (pos_prob - 1.0)[:, None] * reference_unit_vector.astype(jnp.float32)
    )
    block_part = pool
    similarity_table = (
        jnp.einsum(
            "ka,sa->ks", reference_unit_vector, block_part, preferred_element_type=jnp.float32
        )
        / logit_sharpness_divisor
    )
    weights = (jnp.exp(similarity_table - shift_bound) / normalizer[:, None]).astype(jnp.bfloat16)
    grad_neg = lax.psum_scatter(
        reciprocal_factor
        * jnp.einsum(
            "rn,re->ne", weights, reference_unit_vector, preferred_element_type=jnp.float32
        ),
        "batch",
        scatter_dimension=0,
        tiled=True,
    )
    samples = jnp.concatenate([ref_rows, neg_rows, pos_rows], 0)
    animal_ids = jnp.concatenate([ref_animal, neg_animal, ref_animal])
    pre_act = jnp.concatenate([first_enc[0], second_enc[0]], 0)
    hidden = jnp.concatenate([first_enc[1], second_enc[1]], 0)
    latent = jnp.concatenate([first_enc[2], second_enc[2]], 0)
    radius = jnp.concatenate([first_enc[3], second_enc[3]], 0)
    grad_unit = jnp.concatenate([grad_ref, grad_neg, grad_pos], 0)
    inner = jnp.sum(latent * grad_unit, axis=1, keepdims=True)
    grad_latent = ((grad_unit - latent * inner / (radius * radius)) / radius).astype(jnp.bfloat16)
    grad_hidden = jnp.dot(grad_latent, w_out.T, preferred_element_type=jnp.float32)
    grad_pre = jax.vjp(jax.nn.gelu, pre_act)[1](grad_hidden)[0].astype(jnp.bfloat16)
    animals = bias_animal.shape[0]
    animal_hot = (animal_ids[:, None] == jnp.arange(animals, dtype=jnp.int32)[None, :]).astype(
        jnp.bfloat16
    )
    local_in = jnp.dot(samples.T, grad_pre, preferred_element_type=jnp.float32)
    local_out = jnp.dot(hidden.T, grad_latent, preferred_element_type=jnp.float32)
    local_bias = jnp.dot(animal_hot.T, grad_pre, preferred_element_type=jnp.float32)
    grad_w_in, grad_w_out, grad_bias = lax.psum((local_in, local_out, local_bias), ("batch", "tm"))
    return (ref_loss, grad_w_in.astype(jnp.bfloat16), grad_w_out, grad_bias)


def solution(mesh):
    in_specs = (
        P(("batch", "tm"), None),
        P(("batch", "tm"), None),
        P("tm", None),
        P(("batch", "tm"), None),
        P(("batch", "tm")),
        P(("batch", "tm")),
        P(("batch", "tm")),
        P(),
        P(),
        P(),
    )
    out_specs = (P(("batch", "tm")), P(), P(), P())
    return jax.shard_map(
        on_device, mesh=mesh, in_specs=in_specs, out_specs=out_specs, check_vma=False
    )
```

profile of v0, /device:TPU:0, one launch (start us, length us, event | category | flops | bytes accessed | tf_op | source)
XLA Modules:
  0.0 266.8 jit_solution(9246577990645195994)
XLA Ops:
  7.2 0.8 compare_convert_fusion
  8.0 0.6 reduce-window.6
  9.0 0.7 fusion.50
  9.7 0.7 and_reduce_fusion
  10.4 2.1 scatter_custom_fusion
  12.5 4.2 %all-to-all-start = ((s32[2,1,256]{2,1,0:T(1,128)}), s32[2,1,256]{2,1,0:T(1,128)S(1)}, u32[]{:S(2)}, u32[]{:S(2)}) async-start(s32[2,1,256]{2,1,0:T(1,128)} %bitcast.5), calls=%async_computation | async-start | bytes 4096 | tf_op jit(solution)/shard_map/all_to_all | solution.py:67
  16.8 0.7 pad_add_fusion.1
  17.5 1.9 fusion.24
  19.4 1.5 fusion.23
  20.9 0.3 multiply_reduce_fusion.1
  21.3 0.6 copy-done.11
  22.0 22.8 %all_gather.3 = bf16[1024,128]{1,0:T(8,128)(2,1)S(1)} all-gather(bf16[64,128]{1,0:T(8,128)(2,1)S(1)} %slice.22), channel_id=1, replica_groups=mesh['batch'=16,'tm'=2] {'batch'}, dimensions={0}, use_global_device_ids=true | all-gather | bytes 278528 | tf_op jit(solution)/shard_map/all_gather | solution.py:54
  44.9 2.1 gather_fusion
  47.0 1.1 broadcast_select_fusion
  48.1 3.7 %all-to-all-start.1 = ((bf16[2,256,1024]{2,1,0:T(8,128)(2,1)}), bf16[2,256,1024]{2,1,0:T(8,128)(2,1)S(1)}, u32[]{:S(2)}, u32[]{:S(2)}) async-start(bf16[2,256,1024]{2,1,0:T(8,128)(2,1)} %broadcast_select_fusion), calls=%async_computation.1 | async-start | bytes 2097152 | tf_op jit(solution)/shard_map/all_to_all | solution.py:70
  51.9 1.2 fusion.43
  53.2 1.0 fusion.57
  54.1 12.3 %all-to-all-done.1 = bf16[2,256,1024]{2,1,0:T(8,128)(2,1)S(1)} async-done(((bf16[2,256,1024]{2,1,0:T(8,128)(2,1)}), bf16[2,256,1024]{2,1,0:T(8,128)(2,1)S(1)}, u32[]{:S(2)}, u32[]{:S(2)}) %all-to-all-start.1) | async-done | bytes 1048608 | tf_op jit(solution)/shard_map/all_to_all | solution.py:70
  66.5 2.0 gather_fusion.1
  68.4 1.2 broadcast_select_fusion.1
  69.6 2.9 %fusion.39 = (bf16[256,512]{1,0:T(8,128)(2,1)S(1)}, f32[256,512]{1,0:T(8,128)}) fusion(f32[256,512]{1,0:T(8,128)} %fusion.43, bf16[256,1024]{1,0:T(8,128)(2,1)S(1)} %broadcast_select_fusion.1, bf16[1024,512]{1,0:T(8,128)(2,1)} %param.17), kind=kOutput, calls=%fused_computation.54 | convolution fusion | flops 269746176 | bytes 2883584 | tf_op jit(solution)/shard_map/dot_general | solution.py:17
  73.1 0.6 fusion.53
  73.9 1.2 convolution_multiply_fusion.1
  75.2 0.7 pad_add_fusion
  76.4 50.5 %reduce-scatter.2.cloned.1.call-done = f32[64,128]{1,0:T(8,128)} async-done(((f32[1024,128]{1,0:T(8,128)}), f32[64,128]{1,0:T(8,128)}) %reduce-scatter.2.cloned.1.call-update) | async-done | bytes 32784 | tf_op jit(solution)/shard_map/reduce_scatter | solution.py:133
  126.9 0.9 multiply_reduce_fusion
  127.9 2.2 fusion.28
  130.1 2.2 fusion.8
  132.4 1.0 fusion.9
  133.7 69.8 %all-reduce.5 = (bf16[1024,512]{1,0:T(8,128)(2,1)}, f32[8,512]{1,0:T(8,128)}) all-reduce(f32[1024,512]{1,0:T(8,128)S(1)} %fusion.9, f32[8,512]{1,0:T(8,128)S(1)} %fusion.40), channel_id=1, replica_groups=mesh['batch'=16,'tm'=2] {'batch','tm'}, use_global_device_ids=true, to_apply=%region_10.11 | all-reduce | flops 528384 | bytes 3178496 | tf_op jit(solution)/shard_map/psum | solution.py:160
  203.5 54.8 %all-reduce.4.cloned.1.call-done = f32[512,128]{1,0:T(8,128)} async-done(((f32[512,128]{1,0:T(8,128)}), f32[512,128]{1,0:T(8,128)}) %all-reduce.4.cloned.1.call-update) | async-done | bytes 262160 | tf_op jit(solution)/shard_map/psum | solution.py:160
  258.3 1.7 copy.22
  (72 shorter events, 2.4 us)
Async XLA Ops:
  7.2 37.7 %copy-start = (bf16[512,1024]{1,0:T(8,128)(2,1)S(1)}, bf16[512,1024]{1,0:T(8,128)(2,1)}, u32[]{:S(2)}) copy-start(bf16[512,1024]{1,0:T(8,128)(2,1)} %param.12) | copy-start | bytes 3145732
  12.5 32.3 %all-to-all-start = ((s32[2,1,256]{2,1,0:T(1,128)}), s32[2,1,256]{2,1,0:T(1,128)S(1)}, u32[]{:S(2)}, u32[]{:S(2)}) async-start(s32[2,1,256]{2,1,0:T(1,128)} %bitcast.5), calls=%async_computation | async-start | bytes 4096 | tf_op jit(solution)/shard_map/all_to_all | solution.py:67
  17.5 1.9 copy-start.15
  19.4 1.5 copy-start.3
  20.9 1.1 copy-start.7
  21.2 23.7 %copy-start.1 = (f32[320,128]{1,0:T(8,128)}, f32[320,128]{1,0:T(8,128)S(1)}, u32[]{:S(2)}) copy-start(f32[320,128]{1,0:T(8,128)S(1)} %get-tuple-element.52) | copy-start | bytes 491524
  21.3 0.6 copy-start.11
  48.1 3.8 %copy-start.16 = (s32[256]{0:T(256)S(1)}, s32[256]{0:T(256)}, u32[]{:S(2)}) copy-start(s32[256]{0:T(256)} %param.15) | copy-start | bytes 3076
  48.1 18.3 %all-to-all-start.1 = ((bf16[2,256,1024]{2,1,0:T(8,128)(2,1)}), bf16[2,256,1024]{2,1,0:T(8,128)(2,1)S(1)}, u32[]{:S(2)}, u32[]{:S(2)}) async-start(bf16[2,256,1024]{2,1,0:T(8,128)(2,1)} %broadcast_select_fusion), calls=%async_computation.1 | async-start | bytes 2097152 | tf_op jit(solution)/shard_map/all_to_all | solution.py:70
  51.9 75.0 %reduce-scatter.2.cloned.1.call-start = ((), (), s32[]{:S(2)}) async-start(), calls=%async_computation.3 | async-start | bytes 557056 | tf_op jit(solution)/shard_map/reduce_scatter | solution.py:133
  69.6 3.0 %copy-start.5 = (bf16[256,1024]{1,0:T(8,128)(2,1)}, bf16[256,1024]{1,0:T(8,128)(2,1)S(1)}, u32[]{:S(2)}) copy-start(bf16[256,1024]{1,0:T(8,128)(2,1)S(1)} %broadcast_select_fusion.1) | copy-start | bytes 1572868
  69.6 3.0 %copy-start.4 = (bf16[512,128]{1,0:T(8,128)(2,1)S(1)}, bf16[512,128]{1,0:T(8,128)(2,1)}, u32[]{:S(2)}) copy-start(bf16[512,128]{1,0:T(8,128)(2,1)} %param.19) | copy-start | bytes 393220
  69.6 3.5 %copy-start.19 = (f32[256]{0:T(256)S(1)}, f32[256]{0:T(256)}, u32[]{:S(2)}) copy-start(f32[256]{0:T(256)} %get-tuple-element.53) | copy-start | bytes 3076
  72.6 1.3 copy-start.9
  73.9 1.3 copy-start.12
  73.9 1.3 copy-start.17
  73.9 1.3 copy-start.20
  73.9 2.2 copy-start.18
  73.9 53.0 %copy-start.2 = (f32[320,128]{1,0:T(8,128)S(1)}, f32[320,128]{1,0:T(8,128)}, u32[]{:S(2)}) copy-start(f32[320,128]{1,0:T(8,128)} %copy-done.1) | copy-start | bytes 491524
  75.1 52.8 %copy-start.8 = (bf16[320,512]{1,0:T(8,128)(2,1)S(1)}, bf16[320,512]{1,0:T(8,128)(2,1)}, u32[]{:S(2)}) copy-start(bf16[320,512]{1,0:T(8,128)(2,1)} %copy-done.7) | copy-start | bytes 983044
  75.1 52.8 %copy-start.10 = (bf16[256,512]{1,0:T(8,128)(2,1)S(1)}, bf16[256,512]{1,0:T(8,128)(2,1)}, u32[]{:S(2)}) copy-start(bf16[256,512]{1,0:T(8,128)(2,1)} %copy-done.9) | copy-start | bytes 786436
  75.1 183.2 %all-reduce.4.cloned.1.call-start = ((), (), s32[]{:S(2)}) async-start(), calls=%async_computation.4 | async-start | bytes 524288 | tf_op jit(solution)/shard_map/psum | solution.py:160
  127.8 2.2 copy-start.13
  127.9 2.2 copy-start.23
  130.1 2.2 copy-start.6
  130.1 2.2 copy-start.21
  130.1 2.2 copy-start.22
  132.3 1.0 copy-start.14
Sparse Core Ops, SparseCore 0:
  75.2 51.6 reduce-scatter.1
  133.9 124.3 all-reduce.3
where the time goes:
time: 267 us
  waiting for transfers between devices  118 us (44%)
  blocking collectives  92.6 us (35%)
  matrix products  16.3 us (6%)
  between operations  14.5 us (5%)
  other arithmetic  8.99 us (3%)
  local copies, waits for them, and re-layouts  8.77 us (3%)
  starting transfers between devices  8 us (3%)
    psum x1, blocking collectives, on_device(): lax.psum((local_in, local_out, local_bias), ('batch', 'tm'))  69.8 us
    psum x1, waiting for transfers between devices, on_device(): lax.psum((local_in, local_out, local_bias), ('batch', 'tm'))  54.8 us
    reduce_scatter x1, waiting for transfers between devices, on_device(): lax.psum_scatter(reciprocal_factor * jnp.einsum('rn,re->ne', weights, ref...  50.5 us
    all_gather x1, blocking collectives, on_device(): pool = lax.all_gather(neg_unit, 'batch', axis=0, tiled=True)  22.8 us
    all_to_all x1, waiting for transfers between devices, on_device(): lax.all_to_all(found, 'tm', split_axis=0, concat_axis=0, tiled=True)  12.3 us
  transfers between devices with their start and end apart: 4, of which 3 were waited for; matrix products, arithmetic and copies ran while one was open for 4% of the time, Pallas kernels for 0%

commit v1 on v0

--- a/solution.py
+++ b/solution.py
@@ -7,6 +7,22 @@
 logit_sharpness_divisor = 0.1
 shift_bound = 10.0
 epsilon = 1e-06
+
+
+def gather_around(x, axis, dim):
+    ways, here, step = (lax.axis_size(axis), lax.axis_index(axis), x.shape[dim])
+    shape = [n * ways if d == dim else n for d, n in enumerate(x.shape)]
+    full = lax.dynamic_update_slice_in_dim(jnp.zeros(shape, x.dtype), x, here * step, axis=dim)
+    going_up = going_down = x
+    for far in range(1, ways // 2 + 1):
+        going_up = lax.ppermute(going_up, axis, [(d, (d + 1) % ways) for d in range(ways)])
+        full = lax.dynamic_update_slice_in_dim(full, going_up, (here - far) % ways * step, axis=dim)
+        if 2 * far < ways:
+            going_down = lax.ppermute(going_down, axis, [(d, (d - 1) % ways) for d in range(ways)])
+            full = lax.dynamic_update_slice_in_dim(
+                full, going_down, (here + far) % ways * step, axis=dim
+            )
+    return full
 
 
 def encode_rows(samples, animal_ids, w_in, bias_animal, w_out):
@@ -51,7 +67,7 @@
     )
     reference_unit_vector = first_enc[4][:anchors_each_processor]
     neg_unit = first_enc[4][anchors_each_processor:]
-    pool = lax.all_gather(neg_unit, "batch", axis=0, tiled=True)
+    pool = gather_around(neg_unit, "batch", 0)
     owner_ids = pos_owner[:, 0]
     owner_hot = (
         owner_ids[:, None] == jnp.arange(holder_processors, dtype=jnp.int32)[None, :]

time: 267 us -> 280 us (1.049)
  starting transfers between devices: 8 us -> 39 us
  blocking collectives: 92.6 us -> 69.7 us
  waiting for transfers between devices: 118 us -> 124 us
    ppermute x0 -> x15, starting transfers between devices: none -> 32.2 us  [the longest x7 31.6 us: gather_around(): lax.ppermute(going_down, axis, [(d, (d - 1) % ways) for d in range(ways)])]
    all_gather x1 -> x0, blocking collectives: 22.8 us -> none  [on_device(): pool = lax.all_gather(neg_unit, 'batch', axis=0, tiled=True)]
    ppermute x0 -> x15, waiting for transfers between devices: none -> 14.4 us  [the longest x8 14.3 us: gather_around(): lax.ppermute(going_up, axis, [(d, (d + 1) % ways) for d in range(ways)])]
    all_to_all x1, waiting for transfers between devices: 12.3 us -> 0.01 us  [on_device(): lax.all_to_all(found, 'tm', split_axis=0, concat_axis=0, tiled=True)]
  transfers between devices with their start and end apart: 4 -> 19, of which waited for: 3 -> 10; matrix products, arithmetic and copies ran while one was open for 4% -> 5% of each run, Pallas kernels for 0% -> 0%
where the time goes in v1:
time: 280 us
  waiting for transfers between devices  124 us (44%)
  blocking collectives  69.7 us (25%)
  starting transfers between devices  39 us (14%)
  matrix products  16.3 us (6%)
  between operations  14.7 us (5%)
  local copies, waits for them, and re-layouts  9.37 us (3%)
  other arithmetic  6.95 us (2%)
    psum x1, blocking collectives, on_device(): lax.psum((local_in, local_out, local_bias), ('batch', 'tm'))  69.7 us
    psum x1, waiting for transfers between devices, on_device(): lax.psum((local_in, local_out, local_bias), ('batch', 'tm'))  54.7 us
    reduce_scatter x1, waiting for transfers between devices, on_device(): lax.psum_scatter(reciprocal_factor * jnp.einsum('rn,re->ne', weights, ref...  52.1 us
    ppermute x7, starting transfers between devices, gather_around(): lax.ppermute(going_down, axis, [(d, (d - 1) % ways) for d in range(ways)])  31.6 us
    ppermute x8, waiting for transfers between devices, gather_around(): lax.ppermute(going_up, axis, [(d, (d + 1) % ways) for d in range(ways)])  14.3 us
  transfers between devices with their start and end apart: 19, of which 10 were waited for; matrix products, arithmetic and copies ran while one was open for 5% of the time, Pallas kernels for 0%

profile of v1, /device:TPU:0, one launch (start us, length us, event | category | flops | bytes accessed | tf_op | source)
XLA Modules:
  0.0 279.7 jit_solution(14796486481877809702)
XLA Ops:
  8.0 1.9 fusion.24
  10.0 1.5 fusion.23
  13.6 5.1 %collective-permute-start.1 = (bf16[64,128]{1,0:T(8,128)(2,1)S(1)}, bf16[64,128]{1,0:T(8,128)(2,1)S(1)}, u32[]{:S(2)}, u32[]{:S(2)}) collective-permute-start(bf16[64,128]{1,0:T(8,128)(2,1)S(1)} %get-tuple-element.45), channel_id=1, source_target_pairs={{0,30},{2,0},{4,2},{6,4},{8,6},{10,8},{12,10},{14,12},{16,14},{18,... | collective-permute-start | bytes 49160 | tf_op jit(solution)/shard_map/ppermute | solution.py:21
  19.8 2.1 scatter_custom_fusion
  21.9 3.2 %all-to-all-start = ((s32[2,1,256]{2,1,0:T(1,128)}), s32[2,1,256]{2,1,0:T(1,128)S(1)}, u32[]{:S(2)}, u32[]{:S(2)}) async-start(s32[2,1,256]{2,1,0:T(1,128)} %bitcast.5), calls=%async_computation | async-start | bytes 4096 | tf_op jit(solution)/shard_map/all_to_all | solution.py:83
  25.4 1.2 fusion.43
  26.6 2.3 all-to-all-done
  28.9 2.1 gather_fusion
  32.1 3.6 %all-to-all-start.1 = ((bf16[2,256,1024]{2,1,0:T(8,128)(2,1)}), bf16[2,256,1024]{2,1,0:T(8,128)(2,1)S(1)}, u32[]{:S(2)}, u32[]{:S(2)}) async-start(bf16[2,256,1024]{2,1,0:T(8,128)(2,1)} %broadcast_select_fusion), calls=%async_computation.1 | async-start | bytes 2097152 | tf_op jit(solution)/shard_map/all_to_all | solution.py:86
  35.8 4.4 %collective-permute-start.3 = (bf16[64,128]{1,0:T(8,128)(2,1)S(1)}, bf16[64,128]{1,0:T(8,128)(2,1)S(1)}, u32[]{:S(2)}, u32[]{:S(2)}) collective-permute-start(bf16[64,128]{1,0:T(8,128)(2,1)S(1)} %collective-permute-done.1), channel_id=1, source_target_pairs={{0,30},{2,0},{4,2},{6,4},{8,6},{10,8},{12,10},{14,12},{16,14},{18,... | collective-permute-start | bytes 49160 | tf_op jit(solution)/shard_map/ppermute | solution.py:21
  40.3 1.5 collective-permute-done.2
  41.8 4.4 %collective-permute-start.5 = (bf16[64,128]{1,0:T(8,128)(2,1)S(1)}, bf16[64,128]{1,0:T(8,128)(2,1)S(1)}, u32[]{:S(2)}, u32[]{:S(2)}) collective-permute-start(bf16[64,128]{1,0:T(8,128)(2,1)S(1)} %collective-permute-done.3), channel_id=1, source_target_pairs={{0,30},{2,0},{4,2},{6,4},{8,6},{10,8},{12,10},{14,12},{16,14},{18,... | collective-permute-start | bytes 49160 | tf_op jit(solution)/shard_map/ppermute | solution.py:21
  46.2 1.4 collective-permute-done.4
  47.7 4.4 %collective-permute-start.7 = (bf16[64,128]{1,0:T(8,128)(2,1)S(1)}, bf16[64,128]{1,0:T(8,128)(2,1)S(1)}, u32[]{:S(2)}, u32[]{:S(2)}) collective-permute-start(bf16[64,128]{1,0:T(8,128)(2,1)S(1)} %collective-permute-done.5), channel_id=1, source_target_pairs={{0,30},{2,0},{4,2},{6,4},{8,6},{10,8},{12,10},{14,12},{16,14},{18,... | collective-permute-start | bytes 49160 | tf_op jit(solution)/shard_map/ppermute | solution.py:21
  52.1 1.4 collective-permute-done.6
  53.5 4.4 %collective-permute-start.9 = (bf16[64,128]{1,0:T(8,128)(2,1)S(1)}, bf16[64,128]{1,0:T(8,128)(2,1)S(1)}, u32[]{:S(2)}, u32[]{:S(2)}) collective-permute-start(bf16[64,128]{1,0:T(8,128)(2,1)S(1)} %collective-permute-done.7), channel_id=1, source_target_pairs={{0,30},{2,0},{4,2},{6,4},{8,6},{10,8},{12,10},{14,12},{16,14},{18,... | collective-permute-start | bytes 49160 | tf_op jit(solution)/shard_map/ppermute | solution.py:21
  58.0 1.4 collective-permute-done.8
  59.4 4.4 %collective-permute-start.11 = (bf16[64,128]{1,0:T(8,128)(2,1)S(1)}, bf16[64,128]{1,0:T(8,128)(2,1)S(1)}, u32[]{:S(2)}, u32[]{:S(2)}) collective-permute-start(bf16[64,128]{1,0:T(8,128)(2,1)S(1)} %collective-permute-done.9), channel_id=1, source_target_pairs={{0,30},{2,0},{4,2},{6,4},{8,6},{10,8},{12,10},{14,12},{16,14},{18,... | collective-permute-start | bytes 49160 | tf_op jit(solution)/shard_map/ppermute | solution.py:21
  63.8 1.4 collective-permute-done.10
  65.2 4.4 %collective-permute-start.13 = (bf16[64,128]{1,0:T(8,128)(2,1)S(1)}, bf16[64,128]{1,0:T(8,128)(2,1)S(1)}, u32[]{:S(2)}, u32[]{:S(2)}) collective-permute-start(bf16[64,128]{1,0:T(8,128)(2,1)S(1)} %collective-permute-done.11), channel_id=1, source_target_pairs={{0,30},{2,0},{4,2},{6,4},{8,6},{10,8},{12,10},{14,12},{16,14},{18,... | collective-permute-start | bytes 49160 | tf_op jit(solution)/shard_map/ppermute | solution.py:21
  69.7 1.4 collective-permute-done.12
  71.1 5.8 %collective-permute-done.14 = bf16[64,128]{1,0:T(8,128)(2,1)S(1)} collective-permute-done((bf16[64,128]{1,0:T(8,128)(2,1)S(1)}, bf16[64,128]{1,0:T(8,128)(2,1)S(1)}, u32[]{:S(2)}, u32[]{:S(2)}) %collective-permute-start.14) | collective-permute-done | bytes 16416 | tf_op jit(solution)/shard_map/ppermute | solution.py:18
  77.9 2.0 gather_fusion.1
  79.9 1.2 broadcast_select_fusion.1
  81.1 2.9 %fusion.39 = (bf16[256,512]{1,0:T(8,128)(2,1)S(1)}, f32[256,512]{1,0:T(8,128)}) fusion(f32[256,512]{1,0:T(8,128)} %fusion.43, bf16[256,1024]{1,0:T(8,128)(2,1)S(1)} %broadcast_select_fusion.1, bf16[1024,512]{1,0:T(8,128)(2,1)} %param.17), kind=kOutput, calls=%fused_computation.54 | convolution fusion | flops 269746176 | bytes 2883584 | tf_op jit(solution)/shard_map/dot_general | solution.py:33
  85.3 1.1 convolution_multiply_fusion.1
  87.8 52.1 %reduce-scatter.2.cloned.1.call-done = f32[64,128]{1,0:T(8,128)} async-done(((f32[1024,128]{1,0:T(8,128)}), f32[64,128]{1,0:T(8,128)}) %reduce-scatter.2.cloned.1.call-update) | async-done | bytes 32784 | tf_op jit(solution)/shard_map/reduce_scatter | solution.py:149
  141.0 2.2 fusion.28
  143.2 2.2 fusion.8
  146.8 69.7 %all-reduce.5 = (bf16[1024,512]{1,0:T(8,128)(2,1)}, f32[8,512]{1,0:T(8,128)}) all-reduce(f32[1024,512]{1,0:T(8,128)S(1)} %fusion.9, f32[8,512]{1,0:T(8,128)S(1)} %fusion.40), channel_id=1, replica_groups=mesh['batch'=16,'tm'=2] {'batch','tm'}, use_global_device_ids=true, to_apply=%region_10.11 | all-reduce | flops 528384 | bytes 3178496 | tf_op jit(solution)/shard_map/psum | solution.py:176
  216.5 54.7 %all-reduce.4.cloned.1.call-done = f32[512,128]{1,0:T(8,128)} async-done(((f32[512,128]{1,0:T(8,128)}), f32[512,128]{1,0:T(8,128)}) %all-reduce.4.cloned.1.call-update) | async-done | bytes 262160 | tf_op jit(solution)/shard_map/psum | solution.py:176
  271.2 1.7 copy.38
  (119 shorter events, 11.4 us)
Async XLA Ops:
  7.2 21.7 %copy-start = (bf16[512,1024]{1,0:T(8,128)(2,1)S(1)}, bf16[512,1024]{1,0:T(8,128)(2,1)}, u32[]{:S(2)}) copy-start(bf16[512,1024]{1,0:T(8,128)(2,1)} %param.12) | copy-start | bytes 3145732
  9.9 8.7 %copy-start.18 = (s32[256,1]{0,1:T(1,128)S(1)}, s32[256,1]{0,1:T(1,128)}, u32[]{:S(2)}) copy-start(s32[256,1]{0,1:T(1,128)} %param.13) | copy-start | bytes 3076
  11.4 13.9 %copy-start.16 = (s32[256]{0:T(256)S(1)}, s32[256]{0:T(256)}, u32[]{:S(2)}) copy-start(s32[256]{0:T(256)} %param.15) | copy-start | bytes 3076
  13.0 22.7 %collective-permute-start = (bf16[64,128]{1,0:T(8,128)(2,1)S(1)}, bf16[64,128]{1,0:T(8,128)(2,1)S(1)}, u32[]{:S(2)}, u32[]{:S(2)}) collective-permute-start(bf16[64,128]{1,0:T(8,128)(2,1)S(1)} %get-tuple-element.45), channel_id=1, source_target_pairs={{0,2},{2,4},{4,6},{6,8},{8,10},{10,12},{12,14},{14,16},{16,18},{18... | collective-permute-start | bytes 49160 | tf_op jit(solution)/shard_map/ppermute | solution.py:18
  13.6 22.3 %collective-permute-start.1 = (bf16[64,128]{1,0:T(8,128)(2,1)S(1)}, bf16[64,128]{1,0:T(8,128)(2,1)S(1)}, u32[]{:S(2)}, u32[]{:S(2)}) collective-permute-start(bf16[64,128]{1,0:T(8,128)(2,1)S(1)} %get-tuple-element.45), channel_id=1, source_target_pairs={{0,30},{2,0},{4,2},{6,4},{8,6},{10,8},{12,10},{14,12},{16,14},{18,... | collective-permute-start | bytes 49160 | tf_op jit(solution)/shard_map/ppermute | solution.py:21
  21.9 7.0 %all-to-all-start = ((s32[2,1,256]{2,1,0:T(1,128)}), s32[2,1,256]{2,1,0:T(1,128)S(1)}, u32[]{:S(2)}, u32[]{:S(2)}) async-start(s32[2,1,256]{2,1,0:T(1,128)} %bitcast.5), calls=%async_computation | async-start | bytes 4096 | tf_op jit(solution)/shard_map/all_to_all | solution.py:83
  32.1 45.8 %all-to-all-start.1 = ((bf16[2,256,1024]{2,1,0:T(8,128)(2,1)}), bf16[2,256,1024]{2,1,0:T(8,128)(2,1)S(1)}, u32[]{:S(2)}, u32[]{:S(2)}) async-start(bf16[2,256,1024]{2,1,0:T(8,128)(2,1)} %broadcast_select_fusion), calls=%async_computation.1 | async-start | bytes 2097152 | tf_op jit(solution)/shard_map/all_to_all | solution.py:86
  35.7 104.3 %reduce-scatter.2.cloned.1.call-start = ((), (), s32[]{:S(2)}) async-start(), calls=%async_computation.3 | async-start | bytes 557056 | tf_op jit(solution)/shard_map/reduce_scatter | solution.py:149
  35.7 6.0 %collective-permute-start.2 = (bf16[64,128]{1,0:T(8,128)(2,1)S(1)}, bf16[64,128]{1,0:T(8,128)(2,1)S(1)}, u32[]{:S(2)}, u32[]{:S(2)}) collective-permute-start(bf16[64,128]{1,0:T(8,128)(2,1)S(1)} %collective-permute-done), channel_id=1, source_target_pairs={{0,2},{2,4},{4,6},{6,8},{8,10},{10,12},{12,14},{14,16},{16,18},{18... | collective-permute-start | bytes 49160 | tf_op jit(solution)/shard_map/ppermute | solution.py:18
  35.8 5.9 %collective-permute-start.3 = (bf16[64,128]{1,0:T(8,128)(2,1)S(1)}, bf16[64,128]{1,0:T(8,128)(2,1)S(1)}, u32[]{:S(2)}, u32[]{:S(2)}) collective-permute-start(bf16[64,128]{1,0:T(8,128)(2,1)S(1)} %collective-permute-done.1), channel_id=1, source_target_pairs={{0,30},{2,0},{4,2},{6,4},{8,6},{10,8},{12,10},{14,12},{16,14},{18,... | collective-permute-start | bytes 49160 | tf_op jit(solution)/shard_map/ppermute | solution.py:21
  41.8 5.9 %collective-permute-start.4 = (bf16[64,128]{1,0:T(8,128)(2,1)S(1)}, bf16[64,128]{1,0:T(8,128)(2,1)S(1)}, u32[]{:S(2)}, u32[]{:S(2)}) collective-permute-start(bf16[64,128]{1,0:T(8,128)(2,1)S(1)} %collective-permute-done.2), channel_id=1, source_target_pairs={{0,2},{2,4},{4,6},{6,8},{8,10},{10,12},{12,14},{14,16},{16,18},{18... | collective-permute-start | bytes 49160 | tf_op jit(solution)/shard_map/ppermute | solution.py:18
  41.8 5.9 %collective-permute-start.5 = (bf16[64,128]{1,0:T(8,128)(2,1)S(1)}, bf16[64,128]{1,0:T(8,128)(2,1)S(1)}, u32[]{:S(2)}, u32[]{:S(2)}) collective-permute-start(bf16[64,128]{1,0:T(8,128)(2,1)S(1)} %collective-permute-done.3), channel_id=1, source_target_pairs={{0,30},{2,0},{4,2},{6,4},{8,6},{10,8},{12,10},{14,12},{16,14},{18,... | collective-permute-start | bytes 49160 | tf_op jit(solution)/shard_map/ppermute | solution.py:21
  47.6 5.9 %collective-permute-start.6 = (bf16[64,128]{1,0:T(8,128)(2,1)S(1)}, bf16[64,128]{1,0:T(8,128)(2,1)S(1)}, u32[]{:S(2)}, u32[]{:S(2)}) collective-permute-start(bf16[64,128]{1,0:T(8,128)(2,1)S(1)} %collective-permute-done.4), channel_id=1, source_target_pairs={{0,2},{2,4},{4,6},{6,8},{8,10},{10,12},{12,14},{14,16},{16,18},{18... | collective-permute-start | bytes 49160 | tf_op jit(solution)/shard_map/ppermute | solution.py:18
  47.7 5.9 %collective-permute-start.7 = (bf16[64,128]{1,0:T(8,128)(2,1)S(1)}, bf16[64,128]{1,0:T(8,128)(2,1)S(1)}, u32[]{:S(2)}, u32[]{:S(2)}) collective-permute-start(bf16[64,128]{1,0:T(8,128)(2,1)S(1)} %collective-permute-done.5), channel_id=1, source_target_pairs={{0,30},{2,0},{4,2},{6,4},{8,6},{10,8},{12,10},{14,12},{16,14},{18,... | collective-permute-start | bytes 49160 | tf_op jit(solution)/shard_map/ppermute | solution.py:21
  53.5 5.9 %collective-permute-start.8 = (bf16[64,128]{1,0:T(8,128)(2,1)S(1)}, bf16[64,128]{1,0:T(8,128)(2,1)S(1)}, u32[]{:S(2)}, u32[]{:S(2)}) collective-permute-start(bf16[64,128]{1,0:T(8,128)(2,1)S(1)} %collective-permute-done.6), channel_id=1, source_target_pairs={{0,2},{2,4},{4,6},{6,8},{8,10},{10,12},{12,14},{14,16},{16,18},{18... | collective-permute-start | bytes 49160 | tf_op jit(solution)/shard_map/ppermute | solution.py:18
  53.5 5.9 %collective-permute-start.9 = (bf16[64,128]{1,0:T(8,128)(2,1)S(1)}, bf16[64,128]{1,0:T(8,128)(2,1)S(1)}, u32[]{:S(2)}, u32[]{:S(2)}) collective-permute-start(bf16[64,128]{1,0:T(8,128)(2,1)S(1)} %collective-permute-done.7), channel_id=1, source_target_pairs={{0,30},{2,0},{4,2},{6,4},{8,6},{10,8},{12,10},{14,12},{16,14},{18,... | collective-permute-start | bytes 49160 | tf_op jit(solution)/shard_map/ppermute | solution.py:21
  59.3 5.9 %collective-permute-start.10 = (bf16[64,128]{1,0:T(8,128)(2,1)S(1)}, bf16[64,128]{1,0:T(8,128)(2,1)S(1)}, u32[]{:S(2)}, u32[]{:S(2)}) collective-permute-start(bf16[64,128]{1,0:T(8,128)(2,1)S(1)} %collective-permute-done.8), channel_id=1, source_target_pairs={{0,2},{2,4},{4,6},{6,8},{8,10},{10,12},{12,14},{14,16},{16,18},{18... | collective-permute-start | bytes 49160 | tf_op jit(solution)/shard_map/ppermute | solution.py:18
  59.4 5.9 %collective-permute-start.11 = (bf16[64,128]{1,0:T(8,128)(2,1)S(1)}, bf16[64,128]{1,0:T(8,128)(2,1)S(1)}, u32[]{:S(2)}, u32[]{:S(2)}) collective-permute-start(bf16[64,128]{1,0:T(8,128)(2,1)S(1)} %collective-permute-done.9), channel_id=1, source_target_pairs={{0,30},{2,0},{4,2},{6,4},{8,6},{10,8},{12,10},{14,12},{16,14},{18,... | collective-permute-start | bytes 49160 | tf_op jit(solution)/shard_map/ppermute | solution.py:21
  65.2 5.9 %collective-permute-start.12 = (bf16[64,128]{1,0:T(8,128)(2,1)S(1)}, bf16[64,128]{1,0:T(8,128)(2,1)S(1)}, u32[]{:S(2)}, u32[]{:S(2)}) collective-permute-start(bf16[64,128]{1,0:T(8,128)(2,1)S(1)} %collective-permute-done.10), channel_id=1, source_target_pairs={{0,2},{2,4},{4,6},{6,8},{8,10},{10,12},{12,14},{14,16},{16,18},{18... | collective-permute-start | bytes 49160 | tf_op jit(solution)/shard_map/ppermute | solution.py:18
  65.2 5.9 %collective-permute-start.13 = (bf16[64,128]{1,0:T(8,128)(2,1)S(1)}, bf16[64,128]{1,0:T(8,128)(2,1)S(1)}, u32[]{:S(2)}, u32[]{:S(2)}) collective-permute-start(bf16[64,128]{1,0:T(8,128)(2,1)S(1)} %collective-permute-done.11), channel_id=1, source_target_pairs={{0,30},{2,0},{4,2},{6,4},{8,6},{10,8},{12,10},{14,12},{16,14},{18,... | collective-permute-start | bytes 49160 | tf_op jit(solution)/shard_map/ppermute | solution.py:21
  71.1 5.9 %collective-permute-start.14 = (bf16[64,128]{1,0:T(8,128)(2,1)S(1)}, bf16[64,128]{1,0:T(8,128)(2,1)S(1)}, u32[]{:S(2)}, u32[]{:S(2)}) collective-permute-start(bf16[64,128]{1,0:T(8,128)(2,1)S(1)} %collective-permute-done.12), channel_id=1, source_target_pairs={{0,2},{2,4},{4,6},{6,8},{8,10},{10,12},{12,14},{14,16},{16,18},{18... | collective-permute-start | bytes 49160 | tf_op jit(solution)/shard_map/ppermute | solution.py:18
  81.1 3.0 %copy-start.5 = (bf16[256,1024]{1,0:T(8,128)(2,1)}, bf16[256,1024]{1,0:T(8,128)(2,1)S(1)}, u32[]{:S(2)}) copy-start(bf16[256,1024]{1,0:T(8,128)(2,1)S(1)} %broadcast_select_fusion.1) | copy-start | bytes 1572868
  81.1 3.0 %copy-start.4 = (bf16[512,128]{1,0:T(8,128)(2,1)S(1)}, bf16[512,128]{1,0:T(8,128)(2,1)}, u32[]{:S(2)}) copy-start(bf16[512,128]{1,0:T(8,128)(2,1)} %param.19) | copy-start | bytes 393220
  81.1 3.5 %copy-start.20 = (f32[256]{0:T(256)S(1)}, f32[256]{0:T(256)}, u32[]{:S(2)}) copy-start(f32[256]{0:T(256)} %get-tuple-element.55) | copy-start | bytes 3076
  85.3 54.7 %copy-start.2 = (f32[320,128]{1,0:T(8,128)S(1)}, f32[320,128]{1,0:T(8,128)}, u32[]{:S(2)}) copy-start(f32[320,128]{1,0:T(8,128)} %copy-done.1) | copy-start | bytes 491524
  86.5 54.4 %copy-start.8 = (bf16[320,512]{1,0:T(8,128)(2,1)S(1)}, bf16[320,512]{1,0:T(8,128)(2,1)}, u32[]{:S(2)}) copy-start(bf16[320,512]{1,0:T(8,128)(2,1)} %copy-done.7) | copy-start | bytes 983044
  86.5 54.4 %copy-start.10 = (bf16[256,512]{1,0:T(8,128)(2,1)S(1)}, bf16[256,512]{1,0:T(8,128)(2,1)}, u32[]{:S(2)}) copy-start(bf16[256,512]{1,0:T(8,128)(2,1)} %copy-done.9) | copy-start | bytes 786436
  86.5 184.7 %all-reduce.4.cloned.1.call-start = ((), (), s32[]{:S(2)}) async-start(), calls=%async_computation.4 | async-start | bytes 524288 | tf_op jit(solution)/shard_map/psum | solution.py:176
  140.9 2.2 copy-start.13
  140.9 2.2 copy-start.24
  143.2 2.2 copy-start.6
  143.2 2.2 copy-start.22
  (12 other events, 16.0 us)
Sparse Core Ops, SparseCore 0:
  86.6 53.3 reduce-scatter.1
  147.0 124.1 all-reduce.3
